TPU v7x, 128 devices: a whole 4x4x4 slice. The times are simulated.
128 devices in a mesh: agent: 8 (over z, core), chan: 8 (over y, x_hi), batch: 2 (over x_lo).
Axes of the slice: x: 4 (x_hi: 2, x_lo: 2; x = x_hi * 2 + x_lo), y: 4, z: 4, core: 2. Of those that a mesh axis runs over, the one named last changes fastest.
Arguments:
- features: bfloat16 [256, 16, 16384], P(None, None, ('agent', 'chan', 'batch')), may hold values from -6 to 6
- norm_gain: float32 [256], replicated, may hold values from 0.1 to 1.9
- tok_in: bfloat16 [16384, 2048], P('agent'), may hold values from -0.046875 to 0.046875
- tok_out: bfloat16 [2048, 16384], P(None, 'agent'), may hold values from -0.125 to 0.125
- mix_gain: float32 [256], replicated, may hold values from 0.1 to 1.9
- chan_in: bfloat16 [256, 1024], replicated, may hold values from -0.375 to 0.375
- chan_out: bfloat16 [1024, 256], replicated, may hold values from -0.1875 to 0.1875
- head: bfloat16 [256, 8], replicated, may hold values from -8 to 8
- actions: int32 [16, 16384], P(None, ('agent', 'chan', 'batch')), may hold values from 0 to 7
- order: int32 [16384], P(('agent', 'chan', 'batch')), may hold values from 0 to 16383, as said below
Outputs:
- input_grad: float32 [256, 16, 16384], P(None, None, ('agent', 'chan', 'batch'))
- head_grad: float32 [256, 8], replicated
Inputs may be any that keep to these rules, and one draw needn't show every extreme that they name: order maps each aligned block of 128 agents one to one onto the same block.
All inputs are finite; a program needn't handle non-finite values.
Results may differ from a plain program's by a relative error of at most 0.025.
Values may be sent and summed in bfloat16 or wider, within the bound.
A program may use at most 128 MiB of HBM per device.

v0:
```python
import jax
import jax.numpy as jnp
from jax import lax
from jax.sharding import PartitionSpec as P

A = 16384
GELU_K = 0.7978845608028654
GELU_C = 0.044715
EPS = 1e-05


def gelu_value(v):
    return 0.5 * v * (1.0 + jnp.tanh(GELU_K * (v + GELU_C * v * v * v)))


def gelu_slope(v):
    inner = jnp.tanh(GELU_K * (v + GELU_C * v * v * v))
    return 0.5 * (1.0 + inner) + 0.5 * v * (1.0 - inner * inner) * GELU_K * (
        1.0 + 3.0 * GELU_C * v * v
    )


def shaped_gain(gain, field):
    return gain.reshape((gain.shape[0],) + (1,) * (field.ndim - 1))


def norm_forward(field, gain):
    center = jnp.mean(field, axis=0, keepdims=True)
    spread = jnp.mean(jnp.square(field - center), axis=0, keepdims=True)
    scale = lax.rsqrt(spread + EPS)
    unit = (field - center) * scale
    return (unit * shaped_gain(gain, field), unit, scale)


def norm_backward(upstream, gain, unit, scale):
    weighted = upstream * shaped_gain(gain, upstream)
    return scale * (
        weighted
        - jnp.mean(weighted, axis=0, keepdims=True)
        - unit * jnp.mean(weighted * unit, axis=0, keepdims=True)
    )


def to_tokens(field):
    return lax.all_to_all(field, ("chan", "batch"), split_axis=0, concat_axis=2, tiled=True)


def to_channels(field):
    return lax.all_to_all(field, ("chan", "batch"), split_axis=2, concat_axis=0, tiled=True)


def project(weight, hidden_dim, rows):
    agent_dim = 1 - hidden_dim
    partial_sum = lax.dot_general(
        weight, rows, (((agent_dim,), (1,)), ((), ())), preferred_element_type=jnp.float32
    )
    return lax.psum(partial_sum, "agent")


def expand(spread, weight, hidden_dim):
    return lax.dot_general(
        spread, weight, (((0,), (hidden_dim,)), ((), ())), preferred_element_type=jnp.float32
    )


def shards(features, norm_gain, tok_in, tok_out, mix_gain, chan_in, chan_out, head, actions, order):
    wide = features.astype(jnp.float32)
    chans, samples, local = wide.shape
    normed_in, unit_in, scale_in = norm_forward(wide, norm_gain)
    spread_in = to_tokens(normed_in.astype(jnp.bfloat16))
    token_chans, _, agents = spread_in.shape
    token_rows = spread_in.reshape(token_chans * samples, agents)
    hidden_pre = project(tok_in, 1, token_rows)
    hidden_act = gelu_value(hidden_pre).astype(jnp.bfloat16)
    mixed = (
        expand(hidden_act, tok_out, 0).astype(jnp.bfloat16).reshape(token_chans, samples, agents)
    )
    mixed_back = to_channels(mixed)
    first = wide + mixed_back.astype(jnp.float32)
    normed_mid, unit_mid, scale_mid = norm_forward(first, mix_gain)
    flat_mid = normed_mid.astype(jnp.bfloat16).reshape(chans, samples * local)
    inner_pre = lax.dot_general(
        chan_in, flat_mid, (((0,), (0,)), ((), ())), preferred_element_type=jnp.float32
    )
    inner = gelu_value(inner_pre).astype(jnp.bfloat16)
    outer = lax.dot_general(
        chan_out, inner, (((0,), (0,)), ((), ())), preferred_element_type=jnp.float32
    )
    second = (first.reshape(chans, samples * local) + outer).astype(jnp.bfloat16)
    logits = lax.dot_general(
        head, second, (((0,), (0,)), ((), ())), preferred_element_type=jnp.float32
    )
    target = jnp.take_along_axis(actions, (order % local)[None, :], axis=1).reshape(
        1, samples * local
    )
    phases = lax.broadcasted_iota(jnp.int32, logits.shape, 0)
    picked = (phases == target).astype(jnp.float32)
    top = jnp.max(logits, axis=0, keepdims=True)
    exps = jnp.exp(logits - top)
    probs = exps / jnp.sum(exps, axis=0, keepdims=True)
    slope = (probs - picked).astype(jnp.bfloat16)
    head_part = lax.dot_general(
        second, slope, (((1,), (1,)), ((), ())), preferred_element_type=jnp.float32
    )
    head_total = lax.psum(head_part, ("agent", "chan", "batch"))
    head_grad = head_total * (1.0 / (samples * A))
    back_second = lax.dot_general(
        head, slope, (((1,), (0,)), ((), ())), preferred_element_type=jnp.float32
    )
    back_low = back_second.astype(jnp.bfloat16)
    back_inner = lax.dot_general(
        chan_out, back_low, (((1,), (0,)), ((), ())), preferred_element_type=jnp.float32
    )
    back_inner_pre = (back_inner * gelu_slope(inner_pre)).astype(jnp.bfloat16)
    back_mid = lax.dot_general(
        chan_in, back_inner_pre, (((1,), (0,)), ((), ())), preferred_element_type=jnp.float32
    )
    back_first = back_second.reshape(chans, samples, local) + norm_backward(
        back_mid.reshape(chans, samples, local), mix_gain, unit_mid, scale_mid
    )
    back_tokens = to_tokens(back_first.astype(jnp.bfloat16))
    back_rows = back_tokens.reshape(token_chans * samples, agents)
    back_hidden = project(tok_out, 0, back_rows)
    back_hidden_pre = (back_hidden * gelu_slope(hidden_pre)).astype(jnp.bfloat16)
    back_spread = (
        expand(back_hidden_pre, tok_in, 1)
        .astype(jnp.bfloat16)
        .reshape(token_chans, samples, agents)
    )
    back_norm = to_channels(back_spread)
    input_grad = back_first + norm_backward(
        back_norm.astype(jnp.float32), norm_gain, unit_in, scale_in
    )
    return (input_grad, head_grad)


def solution(mesh):
    in_specs = (
        P(None, None, ("agent", "chan", "batch")),
        P(),
        P("agent", None),
        P(None, "agent"),
        P(),
        P(),
        P(),
        P(),
        P(None, ("agent", "chan", "batch")),
        P(("agent", "chan", "batch")),
    )
    out_specs = (P(None, None, ("agent", "chan", "batch")), P())
    return jax.shard_map(shards, mesh=mesh, in_specs=in_specs, out_specs=out_specs, check_vma=False)
```

profile of v0, /device:TPU:1, one launch (start us, length us, event | category | flops | bytes accessed | tf_op | source)
XLA Modules:
  0.0 469.4 jit_solution(13224073951282337597)
XLA Ops:
  10.8 23.5 %all_to_all.48 = bf16[256,16,128]{2,1,0:T(8,128)(2,1)S(1)} all-to-all(bf16[256,16,128]{2,1,0:T(8,128)(2,1)S(1)} %fusion.16), channel_id=1, replica_groups=mesh['agent'=8,'chan'=8,'batch'=2] {'chan','batch'}, dimensions={0} | all-to-all | bytes 2097152 | tf_op jit(solution)/shard_map/all_to_all | solution.py:45
  35.0 7.0 %convolution_bitcast_fusion.1 = f32[2048,256]{0,1:T(8,128)} fusion(bf16[2048,2048]{1,0:T(8,128)(2,1)} %param.12, bf16[32,8,16,128]{3,2,1,0:T(8,128)(2,1)S(1)} %bitcast.134), kind=kOutput, calls=%fused_computation.23 | convolution fusion | flops 2147483648 | bytes 11534336 | tf_op jit(solution)/shard_map/dot_general | solution.py:54
  42.1 64.0 %all-reduce.3.cloned.1.call-done = f32[2048,256]{0,1:T(8,128)} async-done(((f32[2048,256]{0,1:T(8,128)}), f32[2048,256]{0,1:T(8,128)}) %all-reduce.3.cloned.1.call-update) | async-done | bytes 2097168 | tf_op jit(solution)/shard_map/psum | solution.py:57
  106.1 6.6 %convolution_convert_fusion.1 = bf16[256,2048]{1,0:T(8,128)(2,1)S(1)} fusion(bf16[2048,2048]{1,0:T(8,128)(2,1)} %param.13, f32[2048,256]{0,1:T(8,128)} %all-reduce.3.cloned.1.call-done), kind=kOutput, calls=%fused_computation.27 | convolution fusion | flops 2152726528 | bytes 11534336 | tf_op jit(solution)/shard_map/dot_general | solution.py:61
  112.6 8.5 %copy.57 = bf16[16,16,2048]{1,0,2:T(8,128)(2,1)} copy(bf16[16,16,2048]{2,1,0:T(8,128)(2,1)S(1)} %bitcast.133) | data formatting | bytes 2097152 | tf_op jit(solution)/shard_map/reshape | solution.py:76
  121.1 11.2 %reshape.152 = bf16[16,2,16384]{2,1,0:T(2,128)(2,1)} reshape(bf16[2048,16,16]{2,1,0:T(8,128)(2,1)} %bitcast.124) | data formatting | bytes 2097152
  132.4 6.7 %all-to-all-start.1 = ((bf16[16,2,16384]{2,1,0:T(2,128)(2,1)}), bf16[16,2,16384]{2,1,0:T(2,128)(2,1)S(1)}, u32[]{:S(2)}, u32[]{:S(2)}) async-start(bf16[16,2,16384]{2,1,0:T(2,128)(2,1)} %reshape.152), calls=%async_computation.1 | async-start | bytes 2097152 | tf_op jit(solution)/shard_map/all_to_all | solution.py:49
  140.5 13.1 %all-to-all-done.1 = bf16[16,2,16384]{2,1,0:T(2,128)(2,1)S(1)} async-done(((bf16[16,2,16384]{2,1,0:T(2,128)(2,1)}), bf16[16,2,16384]{2,1,0:T(2,128)(2,1)S(1)}, u32[]{:S(2)}, u32[]{:S(2)}) %all-to-all-start.1) | async-done | bytes 1048608 | tf_op jit(solution)/shard_map/all_to_all | solution.py:49
  153.6 7.5 %reshape.153 = bf16[2048,16,16]{2,1,0:T(8,128)(2,1)} reshape(bf16[16,2,16384]{2,1,0:T(2,128)(2,1)S(1)} %all-to-all-done.1) | data formatting | bytes 2097152
  161.1 10.9 %convert_bitcast_fusion = f32[16,16,16,128]{2,1,3,0:T(8,128)} fusion(bf16[16,16,16,128]{1,0,3,2:T(8,128)(2,1)} %bitcast.123), kind=kLoop, calls=%fused_computation.1 | loop fusion | flops 524288 | bytes 3145728 | tf_op jit(solution)/shard_map/convert_element_type | solution.py:79
  172.0 11.4 %copy.58 = f32[16,16,16,128]{3,2,1,0:T(8,128)} copy(f32[16,16,16,128]{2,1,3,0:T(8,128)} %convert_bitcast_fusion) | data formatting | bytes 4194304 | tf_op jit(solution)/shard_map/convert_element_type | solution.py:79
  183.4 2.2 fusion.76
  190.1 3.0 fusion.10
  196.0 9.5 %fusion.29 = (f32[2048]{0:T(1024)S(1)}, f32[2048,256]{1,0:T(8,128)}) fusion(f32[256]{0:T(256)S(1)} %copy-done.13, bf16[256,1024]{1,0:T(8,128)(2,1)S(1)} %copy-done, f32[2048,1024]{1,0:T(8,128)} %copy-done.6, bf16[1024,256]{1,0:T(8,128)(2,1)S(1)} %copy-done.15, f32[2048,256]{1,0:T(8,128)} %fusion.71), kind=kOutput, calls=%fused_computation.48 | convolution fusion | flops 2188376064 | bytes 13640704 | tf_op jit(solution)/shard_map/dot_general | solution.py:115
  205.5 3.1 copy.62
  208.6 3.2 copy.63
  211.8 2.1 multiply_reduce_fusion.1
  214.7 2.1 fusion.75
  216.7 17.1 %all_to_all.49 = bf16[256,16,128]{2,1,0:T(8,128)(2,1)S(1)} all-to-all(bf16[256,16,128]{2,1,0:T(8,128)(2,1)S(1)} %get-tuple-element.2), channel_id=1, replica_groups=mesh['agent'=8,'chan'=8,'batch'=2] {'chan','batch'}, dimensions={0} | all-to-all | bytes 2097152 | tf_op jit(solution)/shard_map/all_to_all | solution.py:45
  234.5 7.0 %convolution_bitcast_fusion = f32[2048,256]{0,1:T(8,128)} fusion(bf16[2048,2048]{1,0:T(8,128)(2,1)} %param.13, bf16[32,8,16,128]{3,2,1,0:T(8,128)(2,1)S(1)} %bitcast.135), kind=kOutput, calls=%fused_computation.22 | convolution fusion | flops 2147483648 | bytes 11534336 | tf_op jit(solution)/shard_map/dot_general | solution.py:54
  241.5 70.8 %all-reduce.5.cloned.1.call-done = f32[2048,256]{0,1:T(8,128)} async-done(((f32[2048,256]{0,1:T(8,128)}), f32[2048,256]{0,1:T(8,128)}) %all-reduce.5.cloned.1.call-update) | async-done | bytes 2097168 | tf_op jit(solution)/shard_map/psum | solution.py:57
  312.3 7.8 %convolution_convert_fusion = bf16[256,2048]{1,0:T(8,128)(2,1)S(1)} fusion(bf16[2048,2048]{1,0:T(8,128)(2,1)} %param.12, f32[2048,256]{0,1:T(8,128)} %all-reduce.5.cloned.1.call-done, f32[2048,256]{0,1:T(8,128)} %all-reduce.3.cloned.1.call-done), kind=kOutput, calls=%fused_computation.26 | convolution fusion | flops 2157969408 | bytes 13631488 | tf_op jit(solution)/shard_map/dot_general | solution.py:61
  320.1 8.5 %copy.65 = bf16[16,16,2048]{1,0,2:T(8,128)(2,1)} copy(bf16[16,16,2048]{2,1,0:T(8,128)(2,1)S(1)} %bitcast.132) | data formatting | bytes 2097152 | tf_op jit(solution)/shard_map/reshape | solution.py:128
  328.6 11.2 %reshape.154 = bf16[16,2,16384]{2,1,0:T(2,128)(2,1)} reshape(bf16[2048,16,16]{2,1,0:T(8,128)(2,1)} %bitcast.125) | data formatting | bytes 2097152
  339.9 6.7 %all-to-all-start.3 = ((bf16[16,2,16384]{2,1,0:T(2,128)(2,1)}), bf16[16,2,16384]{2,1,0:T(2,128)(2,1)S(1)}, u32[]{:S(2)}, u32[]{:S(2)}) async-start(bf16[16,2,16384]{2,1,0:T(2,128)(2,1)} %reshape.154), calls=%async_computation.3 | async-start | bytes 2097152 | tf_op jit(solution)/shard_map/all_to_all | solution.py:49
  346.9 73.3 %psum.23 = f32[256,8]{0,1:T(8,128)S(1)} all-reduce(f32[256,8]{0,1:T(8,128)S(1)} %fusion.69), channel_id=1, replica_groups=mesh['agent'=8,'chan'=8,'batch'=2] {'agent','chan','batch'}, use_global_device_ids=true, to_apply=%region_12.13 | all-reduce | flops 2048 | bytes 16384 | tf_op jit(solution)/shard_map/psum | solution.py:105
  420.8 7.5 %reshape.155 = bf16[2048,16,16]{2,1,0:T(8,128)(2,1)} reshape(bf16[16,2,16384]{2,1,0:T(2,128)(2,1)S(1)} %all-to-all-done.3) | data formatting | bytes 2097152
  428.3 10.9 %convert_bitcast_fusion.1 = f32[16,16,16,128]{2,1,3,0:T(8,128)} fusion(bf16[2048,16,16]{2,1,0:T(8,128)(2,1)} %reshape.155), kind=kLoop, calls=%fused_computation.2 | loop fusion | flops 524288 | bytes 3145728 | tf_op jit(solution)/shard_map/convert_element_type | solution.py:132
  439.2 5.7 %multiply_reduce_fusion = f32[16,128]{0,1:T(8,128)S(1)} fusion(f32[16,16]{1,0:T(8,128)S(1)} %mul.242, bf16[16,16,16,128]{1,0,3,2:T(8,128)(2,1)} %bitcast.122), kind=kLoop, calls=%fused_computation.3 | loop fusion | flops 1570816 | bytes 1057792 | tf_op jit(solution)/shard_map/reduce_sum | solution.py:39
  445.0 11.5 %copy.66 = f32[16,16,16,128]{3,2,1,0:T(8,128)} copy(f32[16,16,16,128]{2,1,3,0:T(8,128)} %convert_bitcast_fusion.1) | data formatting | bytes 4194304 | tf_op jit(solution)/shard_map/convert_element_type | solution.py:132
  456.5 2.2 fusion.17
  458.7 3.6 fusion.20
  (68 shorter events, 15.5 us)
Async XLA Ops:
  7.2 181.3 %copy-start = (bf16[256,1024]{1,0:T(8,128)(2,1)S(1)}, bf16[256,1024]{1,0:T(8,128)(2,1)}, u32[]{:S(2)}) copy-start(bf16[256,1024]{1,0:T(8,128)(2,1)} %param.15) | copy-start | bytes 1572868
  7.2 3.2 copy-start.2
  7.2 3.2 copy-start.12
  7.2 98.9 %all-reduce.3.cloned.1.call-start = ((), (), s32[]{:S(2)}) async-start(), calls=%async_computation.4 | async-start | bytes 4194304 | tf_op jit(solution)/shard_map/psum | solution.py:57
  132.4 7.2 %copy-start.14 = (s32[16,128]{1,0:T(8,128)S(1)}, s32[16,128]{1,0:T(8,128)}, u32[]{:S(2)}) copy-start(s32[16,128]{1,0:T(8,128)} %param.18) | copy-start | bytes 24580
  132.4 7.3 %copy-start.16 = (s32[128]{0:T(128)S(1)}, s32[128]{0:T(128)}, u32[]{:S(2)}) copy-start(s32[128]{0:T(128)} %param.19) | copy-start | bytes 1540
  132.4 21.2 %all-to-all-start.1 = ((bf16[16,2,16384]{2,1,0:T(2,128)(2,1)}), bf16[16,2,16384]{2,1,0:T(2,128)(2,1)S(1)}, u32[]{:S(2)}, u32[]{:S(2)}) async-start(bf16[16,2,16384]{2,1,0:T(2,128)(2,1)} %reshape.152), calls=%async_computation.1 | async-start | bytes 2097152 | tf_op jit(solution)/shard_map/all_to_all | solution.py:49
  139.0 173.2 %all-reduce.5.cloned.1.call-start = ((), (), s32[]{:S(2)}) async-start(), calls=%async_computation.5 | async-start | bytes 4194304 | tf_op jit(solution)/shard_map/psum | solution.py:57
  187.4 0.7 copy-start.13
  188.4 1.6 copy-start.10
  188.5 1.7 copy-start.15
  189.8 3.3 copy-start.6
  190.1 3.0 copy-start.11
  193.2 1.0 copy-start.8
  211.8 2.2 copy-start.4
  211.8 2.8 copy-start.7
  339.9 6.7 %copy-start.9 = (bf16[256,2048]{0,1:T(8,128)(2,1)S(1)}, bf16[256,2048]{0,1:T(8,128)(2,1)}, u32[]{:S(2)}) copy-start(bf16[256,2048]{0,1:T(8,128)(2,1)} %copy-done.8) | copy-start | bytes 3145732
  339.9 80.9 %all-to-all-start.3 = ((bf16[16,2,16384]{2,1,0:T(2,128)(2,1)}), bf16[16,2,16384]{2,1,0:T(2,128)(2,1)S(1)}, u32[]{:S(2)}, u32[]{:S(2)}) async-start(bf16[16,2,16384]{2,1,0:T(2,128)(2,1)} %reshape.154), calls=%async_computation.3 | async-start | bytes 2097152 | tf_op jit(solution)/shard_map/all_to_all | solution.py:49
  444.9 11.5 %copy-start.3 = (bf16[256,16,128]{2,1,0:T(8,128)(2,1)S(1)}, bf16[256,16,128]{2,1,0:T(8,128)(2,1)}, u32[]{:S(2)}) copy-start(bf16[256,16,128]{2,1,0:T(8,128)(2,1)} %param.10) | copy-start | bytes 3145732
  456.5 2.2 copy-start.5
  458.7 3.6 copy-start.1
Sparse Core Ops, SparseCore 0:
  42.2 63.8 all-reduce.2
  241.7 70.5 all-reduce.4
where the time goes:
time: 477 us; the launch traced here: 469 us
  waiting for transfers between devices  148 us (31%)
  blocking collectives  114 us (24%)
  local copies, waits for them, and re-layouts  89.9 us (19%)
  matrix products  44.8 us (9%)
  other arithmetic  44.6 us (9%)
  between operations  14.6 us (3%)
  starting transfers between devices  13.9 us (3%)
    psum x2, waiting for transfers between devices, project(): return lax.psum(partial_sum, 'agent')  135 us
    psum x1, blocking collectives, shards(): head_total = lax.psum(head_part, ('agent', 'chan', 'batch'))  73.3 us
    all_to_all x2, blocking collectives, to_tokens(): lax.all_to_all(field, ('chan', 'batch'), split_axis=0, concat_axis=2, til...  40.6 us
    unnamed x39, local copies, waits for them, and re-layouts  39.6 us
    dot_general x2, matrix products, expand(): lax.dot_general(spread, weight, (((0,), (hidden_dim,)), ((), ())), prefer...  14.4 us
    dot_general x2, matrix products, project(): lax.dot_general(weight, rows, (((agent_dim,), (1,)), ((), ())), preferred...  14.1 us
    all_to_all x2, starting transfers between devices, to_channels(): lax.all_to_all(field, ('chan', 'batch'), split_axis=2, concat_axis=0, til...  13.3 us
    all_to_all x2, waiting for transfers between devices, to_channels(): lax.all_to_all(field, ('chan', 'batch'), split_axis=2, concat_axis=0, til...  13.1 us
  transfers between devices with their start and end apart: 4, of which 3 were waited for; matrix products, arithmetic and copies ran while one was open for 0% of the time, Pallas kernels for 0%

commit v1 on v0

--- a/solution.py
+++ b/solution.py
@@ -2,11 +2,13 @@
 import jax.numpy as jnp
 from jax import lax
 from jax.sharding import PartitionSpec as P
+from jax.lax import psum
 
 A = 16384
 GELU_K = 0.7978845608028654
 GELU_C = 0.044715
 EPS = 1e-05
+indices_arrange = lambda matrix: psum(psum(matrix, axis_name="agent"), ("chan", "batch"))
 
 
 def gelu_value(v):
@@ -102,7 +104,7 @@
     head_part = lax.dot_general(
         second, slope, (((1,), (1,)), ((), ())), preferred_element_type=jnp.float32
     )
-    head_total = lax.psum(head_part, ("agent", "chan", "batch"))
+    head_total = indices_arrange(head_part)
     head_grad = head_total * (1.0 / (samples * A))
     back_second = lax.dot_general(
         head, slope, (((1,), (0,)), ((), ())), preferred_element_type=jnp.float32

time: 477 us -> 453 us (0.950)
  blocking collectives: 114 us -> 89.7 us
    psum x1 -> x2, blocking collectives: 73.3 us -> 49.1 us  [the longest x1 34 us: psum(psum(matrix, axis_name='agent'), ('chan', 'batch'))]
where the time goes in v1:
time: 453 us; the launch traced here: 445 us
  waiting for transfers between devices  148 us (33%)
  local copies, waits for them, and re-layouts  89.7 us (20%)
  blocking collectives  89.7 us (20%)
  matrix products  44.8 us (10%)
  other arithmetic  44.6 us (10%)
  between operations  14.3 us (3%)
  starting transfers between devices  13.6 us (3%)
    psum x2, waiting for transfers between devices, project(): return lax.psum(partial_sum, 'agent')  135 us
    all_to_all x2, blocking collectives, to_tokens(): lax.all_to_all(field, ('chan', 'batch'), split_axis=0, concat_axis=2, til...  40.6 us
    unnamed x39, local copies, waits for them, and re-layouts  39.7 us
    psum x1, blocking collectives, psum(psum(matrix, axis_name='agent'), ('chan', 'batch'))  34 us
    psum x1, blocking collectives, psum(matrix, axis_name='agent')  15.1 us
    dot_general x2, matrix products, expand(): lax.dot_general(spread, weight, (((0,), (hidden_dim,)), ((), ())), prefer...  14.4 us
    dot_general x2, matrix products, project(): lax.dot_general(weight, rows, (((agent_dim,), (1,)), ((), ())), preferred...  14.1 us
    all_to_all x2, waiting for transfers between devices, to_channels(): lax.all_to_all(field, ('chan', 'batch'), split_axis=2, concat_axis=0, til...  13.4 us
  transfers between devices with their start and end apart: 4, of which 3 were waited for; matrix products, arithmetic and copies ran while one was open for 0% of the time, Pallas kernels for 0%

profile of v1, /device:TPU:1, one launch (start us, length us, event | category | flops | bytes accessed | tf_op | source)
XLA Modules:
  0.0 444.8 jit_solution(11546553291443644752)
XLA Ops:
  10.8 23.5 %all_to_all.48 = bf16[256,16,128]{2,1,0:T(8,128)(2,1)S(1)} all-to-all(bf16[256,16,128]{2,1,0:T(8,128)(2,1)S(1)} %fusion.16), channel_id=1, replica_groups=mesh['agent'=8,'chan'=8,'batch'=2] {'chan','batch'}, dimensions={0} | all-to-all | bytes 2097152 | tf_op jit(solution)/shard_map/all_to_all | solution.py:47
  35.0 7.0 %convolution_bitcast_fusion.1 = f32[2048,256]{0,1:T(8,128)} fusion(bf16[2048,2048]{1,0:T(8,128)(2,1)} %param.12, bf16[32,8,16,128]{3,2,1,0:T(8,128)(2,1)S(1)} %bitcast.134), kind=kOutput, calls=%fused_computation.23 | convolution fusion | flops 2147483648 | bytes 11534336 | tf_op jit(solution)/shard_map/dot_general | solution.py:56
  42.1 64.0 %all-reduce.3.cloned.1.call-done = f32[2048,256]{0,1:T(8,128)} async-done(((f32[2048,256]{0,1:T(8,128)}), f32[2048,256]{0,1:T(8,128)}) %all-reduce.3.cloned.1.call-update) | async-done | bytes 2097168 | tf_op jit(solution)/shard_map/psum | solution.py:59
  106.1 6.6 %convolution_convert_fusion.1 = bf16[256,2048]{1,0:T(8,128)(2,1)S(1)} fusion(bf16[2048,2048]{1,0:T(8,128)(2,1)} %param.13, f32[2048,256]{0,1:T(8,128)} %all-reduce.3.cloned.1.call-done), kind=kOutput, calls=%fused_computation.27 | convolution fusion | flops 2152726528 | bytes 11534336 | tf_op jit(solution)/shard_map/dot_general | solution.py:63
  112.6 8.5 %copy.57 = bf16[16,16,2048]{1,0,2:T(8,128)(2,1)} copy(bf16[16,16,2048]{2,1,0:T(8,128)(2,1)S(1)} %bitcast.133) | data formatting | bytes 2097152 | tf_op jit(solution)/shard_map/reshape | solution.py:78
  121.1 11.2 %reshape.152 = bf16[16,2,16384]{2,1,0:T(2,128)(2,1)} reshape(bf16[2048,16,16]{2,1,0:T(8,128)(2,1)} %bitcast.124) | data formatting | bytes 2097152
  132.4 6.7 %all-to-all-start.1 = ((bf16[16,2,16384]{2,1,0:T(2,128)(2,1)}), bf16[16,2,16384]{2,1,0:T(2,128)(2,1)S(1)}, u32[]{:S(2)}, u32[]{:S(2)}) async-start(bf16[16,2,16384]{2,1,0:T(2,128)(2,1)} %reshape.152), calls=%async_computation.1 | async-start | bytes 2097152 | tf_op jit(solution)/shard_map/all_to_all | solution.py:51
  140.2 13.4 %all-to-all-done.1 = bf16[16,2,16384]{2,1,0:T(2,128)(2,1)S(1)} async-done(((bf16[16,2,16384]{2,1,0:T(2,128)(2,1)}), bf16[16,2,16384]{2,1,0:T(2,128)(2,1)S(1)}, u32[]{:S(2)}, u32[]{:S(2)}) %all-to-all-start.1) | async-done | bytes 1048608 | tf_op jit(solution)/shard_map/all_to_all | solution.py:51
  153.6 7.5 %reshape.153 = bf16[2048,16,16]{2,1,0:T(8,128)(2,1)} reshape(bf16[16,2,16384]{2,1,0:T(2,128)(2,1)S(1)} %all-to-all-done.1) | data formatting | bytes 2097152
  161.1 10.9 %convert_bitcast_fusion = f32[16,16,16,128]{2,1,3,0:T(8,128)} fusion(bf16[16,16,16,128]{1,0,3,2:T(8,128)(2,1)} %bitcast.123), kind=kLoop, calls=%fused_computation.1 | loop fusion | flops 524288 | bytes 3145728 | tf_op jit(solution)/shard_map/convert_element_type | solution.py:81
  172.0 11.4 %copy.58 = f32[16,16,16,128]{3,2,1,0:T(8,128)} copy(f32[16,16,16,128]{2,1,3,0:T(8,128)} %convert_bitcast_fusion) | data formatting | bytes 4194304 | tf_op jit(solution)/shard_map/convert_element_type | solution.py:81
  183.4 2.2 fusion.76
  190.1 3.0 fusion.10
  196.0 9.5 %fusion.29 = (f32[2048]{0:T(1024)S(1)}, f32[2048,256]{1,0:T(8,128)}) fusion(f32[256]{0:T(256)S(1)} %copy-done.13, bf16[256,1024]{1,0:T(8,128)(2,1)S(1)} %copy-done, f32[2048,1024]{1,0:T(8,128)} %copy-done.6, bf16[1024,256]{1,0:T(8,128)(2,1)S(1)} %copy-done.15, f32[2048,256]{1,0:T(8,128)} %fusion.71), kind=kOutput, calls=%fused_computation.48 | convolution fusion | flops 2188376064 | bytes 13640704 | tf_op jit(solution)/shard_map/dot_general | solution.py:117
  205.5 3.1 copy.62
  208.6 3.0 copy.63
  211.7 2.1 multiply_reduce_fusion.1
  216.6 17.1 %all_to_all.49 = bf16[256,16,128]{2,1,0:T(8,128)(2,1)S(1)} all-to-all(bf16[256,16,128]{2,1,0:T(8,128)(2,1)S(1)} %get-tuple-element.2), channel_id=1, replica_groups=mesh['agent'=8,'chan'=8,'batch'=2] {'chan','batch'}, dimensions={0} | all-to-all | bytes 2097152 | tf_op jit(solution)/shard_map/all_to_all | solution.py:47
  234.3 7.0 %convolution_bitcast_fusion = f32[2048,256]{0,1:T(8,128)} fusion(bf16[2048,2048]{1,0:T(8,128)(2,1)} %param.13, bf16[32,8,16,128]{3,2,1,0:T(8,128)(2,1)S(1)} %bitcast.135), kind=kOutput, calls=%fused_computation.22 | convolution fusion | flops 2147483648 | bytes 11534336 | tf_op jit(solution)/shard_map/dot_general | solution.py:56
  241.4 70.7 %all-reduce.5.cloned.1.call-done = f32[2048,256]{0,1:T(8,128)} async-done(((f32[2048,256]{0,1:T(8,128)}), f32[2048,256]{0,1:T(8,128)}) %all-reduce.5.cloned.1.call-update) | async-done | bytes 2097168 | tf_op jit(solution)/shard_map/psum | solution.py:59
  312.1 7.8 %convolution_convert_fusion = bf16[256,2048]{1,0:T(8,128)(2,1)S(1)} fusion(bf16[2048,2048]{1,0:T(8,128)(2,1)} %param.12, f32[2048,256]{0,1:T(8,128)} %all-reduce.5.cloned.1.call-done, f32[2048,256]{0,1:T(8,128)} %all-reduce.3.cloned.1.call-done), kind=kOutput, calls=%fused_computation.26 | convolution fusion | flops 2157969408 | bytes 13631488 | tf_op jit(solution)/shard_map/dot_general | solution.py:63
  319.9 8.5 %copy.65 = bf16[16,16,2048]{1,0,2:T(8,128)(2,1)} copy(bf16[16,16,2048]{2,1,0:T(8,128)(2,1)S(1)} %bitcast.132) | data formatting | bytes 2097152 | tf_op jit(solution)/shard_map/reshape | solution.py:130
  328.4 11.2 %reshape.154 = bf16[16,2,16384]{2,1,0:T(2,128)(2,1)} reshape(bf16[2048,16,16]{2,1,0:T(8,128)(2,1)} %bitcast.125) | data formatting | bytes 2097152
  339.7 6.7 %all-to-all-start.3 = ((bf16[16,2,16384]{2,1,0:T(2,128)(2,1)}), bf16[16,2,16384]{2,1,0:T(2,128)(2,1)S(1)}, u32[]{:S(2)}, u32[]{:S(2)}) async-start(bf16[16,2,16384]{2,1,0:T(2,128)(2,1)} %reshape.154), calls=%async_computation.3 | async-start | bytes 2097152 | tf_op jit(solution)/shard_map/all_to_all | solution.py:51
  346.7 15.1 %psum.30 = f32[256,8]{0,1:T(8,128)S(1)} all-reduce(f32[256,8]{0,1:T(8,128)S(1)} %fusion.69), channel_id=1, replica_groups=mesh['agent'=8,'chan'=8,'batch'=2] {'agent'}, use_global_device_ids=true, to_apply=%region_12.13 | all-reduce | flops 2048 | bytes 16384 | tf_op jit(solution)/shard_map/psum | solution.py:11
  361.8 34.0 %psum.31 = f32[256,8]{0,1:T(8,128)S(1)} all-reduce(f32[256,8]{0,1:T(8,128)S(1)} %psum.30), channel_id=1, replica_groups=mesh['agent'=8,'chan'=8,'batch'=2] {'chan','batch'}, use_global_device_ids=true, to_apply=%region_13.14 | all-reduce | flops 2048 | bytes 16384 | tf_op jit(solution)/shard_map/psum | solution.py:11
  396.4 7.5 %reshape.155 = bf16[2048,16,16]{2,1,0:T(8,128)(2,1)} reshape(bf16[16,2,16384]{2,1,0:T(2,128)(2,1)S(1)} %all-to-all-done.3) | data formatting | bytes 2097152
  403.9 10.9 %convert_bitcast_fusion.1 = f32[16,16,16,128]{2,1,3,0:T(8,128)} fusion(bf16[2048,16,16]{2,1,0:T(8,128)(2,1)} %reshape.155), kind=kLoop, calls=%fused_computation.2 | loop fusion | flops 524288 | bytes 3145728 | tf_op jit(solution)/shard_map/convert_element_type | solution.py:134
  414.8 5.7 %multiply_reduce_fusion = f32[16,128]{0,1:T(8,128)S(1)} fusion(f32[16,16]{1,0:T(8,128)S(1)} %mul.242, bf16[16,16,16,128]{1,0,3,2:T(8,128)(2,1)} %bitcast.122), kind=kLoop, calls=%fused_computation.3 | loop fusion | flops 1570816 | bytes 1057792 | tf_op jit(solution)/shard_map/reduce_sum | solution.py:41
  420.6 11.5 %copy.66 = f32[16,16,16,128]{3,2,1,0:T(8,128)} copy(f32[16,16,16,128]{2,1,3,0:T(8,128)} %convert_bitcast_fusion.1) | data formatting | bytes 4194304 | tf_op jit(solution)/shard_map/convert_element_type | solution.py:134
  432.1 2.2 fusion.17
  434.4 3.6 fusion.20
  (69 shorter events, 17.3 us)
Async XLA Ops:
  7.2 181.3 %copy-start = (bf16[256,1024]{1,0:T(8,128)(2,1)S(1)}, bf16[256,1024]{1,0:T(8,128)(2,1)}, u32[]{:S(2)}) copy-start(bf16[256,1024]{1,0:T(8,128)(2,1)} %param.15) | copy-start | bytes 1572868
  7.2 3.2 copy-start.2
  7.2 3.2 copy-start.12
  7.2 98.9 %all-reduce.3.cloned.1.call-start = ((), (), s32[]{:S(2)}) async-start(), calls=%async_computation.4 | async-start | bytes 4194304 | tf_op jit(solution)/shard_map/psum | solution.py:59
  132.4 6.9 %copy-start.14 = (s32[16,128]{1,0:T(8,128)S(1)}, s32[16,128]{1,0:T(8,128)}, u32[]{:S(2)}) copy-start(s32[16,128]{1,0:T(8,128)} %param.18) | copy-start | bytes 24580
  132.4 7.0 %copy-start.16 = (s32[128]{0:T(128)S(1)}, s32[128]{0:T(128)}, u32[]{:S(2)}) copy-start(s32[128]{0:T(128)} %param.19) | copy-start | bytes 1540
  132.4 21.2 %all-to-all-start.1 = ((bf16[16,2,16384]{2,1,0:T(2,128)(2,1)}), bf16[16,2,16384]{2,1,0:T(2,128)(2,1)S(1)}, u32[]{:S(2)}, u32[]{:S(2)}) async-start(bf16[16,2,16384]{2,1,0:T(2,128)(2,1)} %reshape.152), calls=%async_computation.1 | async-start | bytes 2097152 | tf_op jit(solution)/shard_map/all_to_all | solution.py:51
  139.0 173.0 %all-reduce.5.cloned.1.call-start = ((), (), s32[]{:S(2)}) async-start(), calls=%async_computation.5 | async-start | bytes 4194304 | tf_op jit(solution)/shard_map/psum | solution.py:59
  187.4 0.7 copy-start.13
  188.5 1.6 copy-start.10
  188.5 1.7 copy-start.15
  189.8 3.3 copy-start.6
  190.1 3.0 copy-start.11
  193.2 1.0 copy-start.8
  211.7 2.2 copy-start.4
  211.7 2.9 copy-start.7
  339.7 6.8 %copy-start.9 = (bf16[256,2048]{0,1:T(8,128)(2,1)S(1)}, bf16[256,2048]{0,1:T(8,128)(2,1)}, u32[]{:S(2)}) copy-start(bf16[256,2048]{0,1:T(8,128)(2,1)} %copy-done.8) | copy-start | bytes 3145732
  339.7 56.7 %all-to-all-start.3 = ((bf16[16,2,16384]{2,1,0:T(2,128)(2,1)}), bf16[16,2,16384]{2,1,0:T(2,128)(2,1)S(1)}, u32[]{:S(2)}, u32[]{:S(2)}) async-start(bf16[16,2,16384]{2,1,0:T(2,128)(2,1)} %reshape.154), calls=%async_computation.3 | async-start | bytes 2097152 | tf_op jit(solution)/shard_map/all_to_all | solution.py:51
  420.6 11.5 %copy-start.3 = (bf16[256,16,128]{2,1,0:T(8,128)(2,1)S(1)}, bf16[256,16,128]{2,1,0:T(8,128)(2,1)}, u32[]{:S(2)}) copy-start(bf16[256,16,128]{2,1,0:T(8,128)(2,1)} %param.10) | copy-start | bytes 3145732
  432.1 2.2 copy-start.5
  434.3 3.6 copy-start.1
Sparse Core Ops, SparseCore 0:
  42.2 63.8 all-reduce.2
  241.5 70.5 all-reduce.4
